TPU v7x, 128 devices: a whole 4x4x4 slice. The times are simulated.
128 devices in a mesh: polar: 16 (over x_hi, y, core), azimuth: 8 (over x_lo, z).
Axes of the slice: x: 4 (x_hi: 2, x_lo: 2; x = x_hi * 2 + x_lo), y: 4, z: 4, core: 2. Of those that a mesh axis runs over, the one named last changes fastest.
Arguments:
- grid_input: bfloat16 [720, 276480], P('polar', 'azimuth'), may hold values from -6 to 6
- cotangent: bfloat16 [720, 192, 1440], P('polar', 'azimuth'), may hold values from -6 to 6
- forward_legendre: bfloat16 [720, 256, 256], P(None, 'polar'), may hold values from -0.21875 to 0.21875
- inverse_legendre: bfloat16 [720, 256, 256], P(None, 'polar'), may hold values from -0.375 to 0.375
- filter_weight: bfloat16 [256, 73728], P('polar'), may hold values from -0.3125 to 0.3125
Outputs:
- filtered: bfloat16 [720, 192, 1440], P('polar', 'azimuth')
- grid_grad: bfloat16 [720, 276480], P('polar', 'azimuth')
All inputs are finite; a program needn't handle non-finite values.
Results may differ from a plain program's by a relative error of at most 0.02.
Values may be sent and summed in bfloat16 or wider, within the bound.
No kernel may reach another device: no remote copies, remote signals or barrier semaphores. Data moves between devices by JAX's collectives and lax.ppermute only.
A program may use at most 256 MiB of HBM per device.

v0:
```python
import functools
import math
import numpy as np
import ml_dtypes
import jax
import jax.numpy as jnp
from jax import lax
from jax.sharding import PartitionSpec as P
from jax.experimental import pallas as pl
from jax.experimental.pallas import tpu as pltpu

LAT = 720
LON = 1440
C = 192
DEG = 256
ORD = 256
ORDER_A = (0, 1, 3, 7, 6, 5, 4, 2)
ORDER_E = (0, 7, 6, 1, 3, 5, 4, 2)
NP = 16
NA = 8
ROWS = 45
SLOTS = 6
PAIRS = 90
LP = 96
W = 1152
F32 = jnp.float32
BF = jnp.bfloat16


def params():
    return pltpu.CompilerParams(vmem_limit_bytes=56 << 20)


def dot(a, b, ca, cb):
    return lax.dot_general(a, b, (((ca,), (cb,)), ((), ())), preferred_element_type=F32)


def tables():
    lon = np.arange(LON)[:, None]
    m = np.arange(ORD)[None, :]
    ang = ((lon * m) % LON) * (2.0 * math.pi / LON)
    fac = 1.0 / math.sqrt(LON)
    st = np.stack([np.cos(ang) * fac, -np.sin(ang) * fac], axis=-1).astype(np.float32)
    dbl = np.where(np.arange(ORD) == 0, 1.0, 2.0).astype(np.float32)[None, :, None]
    plain = st.reshape(LON, 2 * ORD).astype(ml_dtypes.bfloat16)
    doubled = (st * dbl).reshape(LON, 2 * ORD).astype(ml_dtypes.bfloat16)
    p4 = plain.reshape(NA, PAIRS, 2, 2 * ORD).transpose(2, 0, 1, 3)
    pp = np.zeros((2, NA, LP, 2 * ORD), ml_dtypes.bfloat16)
    pp[:, :, :PAIRS] = p4
    pp = pp.reshape(2 * NA * LP, 2 * ORD)
    return np.ascontiguousarray(doubled.T), np.ascontiguousarray(pp.T), pp


def prep_body(me_ref, x_ref, *refs):
    outs, s_ref = refs[:8], refs[8]
    step = pl.program_id(0)
    me = me_ref[0]
    lane = lax.broadcasted_iota(jnp.int32, (8, 6144), 1) + step * 6144
    good = lane < PAIRS * 384
    for k in range(SLOTS):
        if k < 5:
            v = x_ref[8 * k:8 * k + 8, :].astype(F32)
        else:
            v = jnp.concatenate([x_ref[40:45, :].astype(F32), jnp.zeros((3, 6144), F32)], 0)
        v = jnp.where(good, v, 0.0)
        for lp in range(16):
            for t in range(3):
                s_ref[3 * k + t, pl.ds(lp, 8, stride=16), :] = v[:, (3 * lp + t) * 128:(3 * lp + t + 1) * 128]
    for s in range(NA):
        row = pl.multiple_of(16 * (me ^ ORDER_A[s]), 16)
        for q in range(18):
            outs[s][:, q * 128:(q + 1) * 128] = s_ref[q, pl.ds(row, 16), :].astype(BF)


def prep(me, x):
    return pl.pallas_call(
        prep_body,
        grid_spec=pltpu.PrefetchScalarGridSpec(
            num_scalar_prefetch=1,
            grid=(6,),
            in_specs=[pl.BlockSpec((ROWS, 6144), lambda i, me: (0, i))],
            out_specs=[pl.BlockSpec((16, 2304), lambda i, me: (i, 0))] * NA,
            scratch_shapes=[pltpu.VMEM((18, 128, 128), F32)],
        ),
        out_shape=[jax.ShapeDtypeStruct((LP, 2304), BF)] * NA,
        compiler_params=params(),
        name="prep",
    )(me, x)


def post_body(me_ref, *refs):
    r_refs, o_ref, s_ref = refs[:8], refs[8], refs[9]
    me = me_ref[0]
    for s in range(NA):
        row = pl.multiple_of(16 * (me ^ ORDER_E[s]), 16)
        for q in range(18):
            s_ref[q, pl.ds(row, 16), :] = r_refs[s][:, q * 128:(q + 1) * 128].astype(F32)
    for k in range(SLOTS):
        for lp in range(16):
            for t in range(3):
                v = s_ref[3 * k + t, pl.ds(lp, 8, stride=16), :].astype(BF)
                n = 8 if k < 5 else 5
                o_ref[8 * k:8 * k + n, (3 * lp + t) * 128:(3 * lp + t + 1) * 128] = v[:n]


def post(me, pieces):
    return pl.pallas_call(
        post_body,
        grid_spec=pltpu.PrefetchScalarGridSpec(
            num_scalar_prefetch=1,
            grid=(6,),
            in_specs=[pl.BlockSpec((16, 2304), lambda i, me: (i, 0))] * NA,
            out_specs=pl.BlockSpec((ROWS, 6144), lambda i, me: (0, i)),
            scratch_shapes=[pltpu.VMEM((18, 128, 128), F32)],
        ),
        out_shape=jax.ShapeDtypeStruct((ROWS, LON // NA * C), BF),
        compiler_params=params(),
        name="post",
    )(me, *pieces)


def whole(body, out, *args, scratch=(), name=None):
    return pl.pallas_call(
        body,
        out_shape=jax.ShapeDtypeStruct(out, BF),
        scratch_shapes=list(scratch),
        compiler_params=params(),
        name=name,
    )(*args)


def dft_f_body(me_ref, *refs):
    r_refs, b_ref, o_ref, x_ref = refs[:8], refs[8], refs[9], refs[10]
    me = me_ref[0]
    for s in range(NA):
        row = pl.multiple_of(LP * (me ^ ORDER_A[s]), 32)
        for k in range(SLOTS):
            v = r_refs[s][:, 384 * k:384 * k + 384]
            x_ref[pl.ds(row, LP), C * k:C * k + C] = v[:, :C]
            x_ref[pl.ds(768 + row, LP), C * k:C * k + C] = v[:, C:]
    y = dot(b_ref[...], x_ref[...], 1, 0).astype(BF)
    o_ref[...] = y.reshape(128, 4, W)


SMEM = pl.BlockSpec(memory_space=pltpu.SMEM)
VMEM = pl.BlockSpec(memory_space=pltpu.VMEM)


def dft_f(me, pieces, bpt):
    return pl.pallas_call(
        dft_f_body,
        in_specs=[SMEM] + [VMEM] * 9,
        out_shape=jax.ShapeDtypeStruct((128, 4, W), BF),
        scratch_shapes=[pltpu.VMEM((1536, W), BF)],
        compiler_params=params(),
        name="dft_f",
    )(me, *pieces, bpt)


def dft_g_body(x_ref, b_ref, o_ref):
    y = dot(b_ref[...], x_ref[...], 1, 1).astype(BF)
    y = jnp.concatenate([y, jnp.zeros((512, W - 1080), BF)], 1)
    o_ref[...] = y.reshape(128, 4, W)


def dft_g(x, bdt):
    return whole(dft_g_body, (128, 4, W), x, bdt, name="dft_g")


def leg_f_body(r_ref, p_ref, o_ref, s_ref):
    for m in range(2):
        for r in range(2):
            v = r_ref[:, 2 * m + r, :]
            for k in range(SLOTS):
                s_ref[128 * k:128 * k + 128, C * r:C * r + C] = v[:, C * k:C * k + C]
        y = dot(p_ref[m], s_ref[...], 0, 0).astype(BF)
        o_ref[:, 384 * m:384 * m + 384] = y


def leg_f(r, pf):
    return whole(leg_f_body, (DEG, 768), r, pf, scratch=[pltpu.VMEM((768, 384), BF)], name="leg_f")


def leg_g_body(r_ref, p_ref, o_ref, s_ref):
    for m in range(2):
        for r in range(2):
            v = r_ref[:, 2 * m + r, :].astype(F32).reshape(NP, NA, W)
            for a in range(NA):
                va = v[:, a, :].astype(BF)
                for t in range(48):
                    s_ref[16 * t:16 * t + 16, C * r + 24 * a:C * r + 24 * a + 24] = va[:, 24 * t:24 * t + 24]
        y = dot(p_ref[m], s_ref[...], 0, 0).astype(BF)
        o_ref[:, 384 * m:384 * m + 384] = y


def leg_g(r, pi):
    return whole(leg_g_body, (DEG, 768), r, pi, scratch=[pltpu.VMEM((768, 384), BF)], name="leg_g")


def mix_body(adjoint, r_ref, k_ref, o_ref, s_ref):
    i = lax.broadcasted_iota(jnp.int32, (256, 256), 0)
    j = lax.broadcasted_iota(jnp.int32, (256, 256), 1)
    perm = ((i // 16 == j % 16) & (i % 16 == j // 16)).astype(F32).astype(BF)
    x = dot(perm, r_ref[...].reshape(256, 768), 1, 0).astype(BF)
    for l in range(16):
        v = x[16 * l:16 * l + 16]
        v = jnp.concatenate([v[:, :384], v[:, 384:]], 0)
        y = dot(v, k_ref[l], 1, 1 if adjoint else 0).astype(BF)
        s_ref[16 * l:16 * l + 16, :384] = y[:16]
        s_ref[16 * l:16 * l + 16, 384:] = y[16:]
    o_ref[...] = dot(perm, s_ref[...], 1, 0).astype(BF).reshape(16, 16, 768)


def mix(r, k, adjoint):
    return whole(functools.partial(mix_body, adjoint), (16, 16, 768), r, k, scratch=[pltpu.VMEM((256, 768), BF)], name="mix_g" if adjoint else "mix_f")


def syn_f_body(x_ref, p_ref, o_ref, z_ref):
    for m in range(2):
        y = dot(p_ref[m], x_ref[:, 384 * m:384 * m + 384], 1, 0).astype(BF)
        for r in range(2):
            for a in range(NA):
                for t in range(48):
                    z_ref[a, :, 24 * t:24 * t + 24] = y[16 * t:16 * t + 16, C * r + 24 * a:C * r + 24 * a + 24]
            for p in range(NP):
                o_ref[8 * p:8 * p + 8, 2 * m + r, :] = z_ref[:, p, :]


def syn_f(x, pi):
    return whole(syn_f_body, (128, 4, W), x, pi, scratch=[pltpu.VMEM((8, 16, W), BF)], name="syn_f")


def syn_g_body(x_ref, p_ref, o_ref, z_ref):
    for m in range(2):
        y = dot(p_ref[m], x_ref[:, 384 * m:384 * m + 384], 1, 0).astype(BF)
        for r in range(2):
            for k in range(SLOTS):
                z_ref[:, C * k:C * k + C] = y[128 * k:128 * k + 128, C * r:C * r + C]
            o_ref[:, 2 * m + r, :] = z_ref[...]


def syn_g(x, pf):
    return whole(syn_g_body, (128, 4, W), x, pf, scratch=[pltpu.VMEM((128, W), BF)], name="syn_g")


def idft_f_body(y_ref, b_ref, o_ref):
    y = y_ref[...].reshape(512, W)
    o_ref[...] = dot(y[:, :1080], b_ref[...], 0, 0).astype(BF)


def idft_f(y, bdt):
    return whole(idft_f_body, (1080, LON), y, bdt, name="idft_f")


def idft_g_body(me_ref, y_ref, b_ref, *refs):
    outs, z_ref = refs[:8], refs[8]
    me = me_ref[0]
    y = y_ref[...].reshape(512, W)
    z_ref[...] = dot(b_ref[...], y, 1, 0).astype(BF)
    for s in range(NA):
        row = pl.multiple_of(LP * (me ^ ORDER_E[s]), 32)
        for k in range(SLOTS):
            e = z_ref[pl.ds(row, LP), C * k:C * k + C]
            o = z_ref[pl.ds(768 + row, LP), C * k:C * k + C]
            outs[s][:, 384 * k:384 * k + 384] = jnp.concatenate([e, o], 1)


def idft_g(me, y, bp):
    return pl.pallas_call(
        idft_g_body,
        in_specs=[SMEM, VMEM, VMEM],
        out_shape=[jax.ShapeDtypeStruct((LP, 2304), BF)] * NA,
        out_specs=[VMEM] * NA,
        scratch_shapes=[pltpu.VMEM((1536, W), BF)],
        compiler_params=params(),
        name="idft_g",
    )(me, y, bp)


def order_tables(table, first):
    part = lax.dynamic_slice(table, (0, first, 0), (LAT, 2, DEG))
    part = part.reshape(NP, ROWS, 2, DEG).transpose(2, 0, 1, 3)
    return jnp.pad(part, ((0, 0), (0, 0), (0, 3), (0, 0)))


def hops(pieces, order):
    def hop(piece, s):
        return lax.ppermute(piece, "azimuth", [(a, a ^ s) for a in range(NA)])

    return [pieces[0]] + [hop(pieces[i], order[i]) for i in range(1, NA)]


def fence(*values):
    return lax.optimization_barrier(values)


def on_device(grid_input, cotangent, forward_legendre, inverse_legendre, filter_weight):
    bdt, bpt, bp = [jnp.asarray(t) for t in tables()]
    both = ("polar", "azimuth")
    me = lax.axis_index("azimuth")[None]
    first = 2 * me[0]

    def over_all(x):
        return lax.all_to_all(x, both, 0, 0)

    def over_polar(x):
        return lax.all_to_all(x, "polar", 0, 0)

    pieces = list(prep(me, grid_input))
    got = hops(pieces, ORDER_A)

    pf = order_tables(forward_legendre, first)
    pf = pf.reshape(2, NP, SLOTS, NA, DEG).transpose(0, 2, 1, 3, 4).reshape(2, 768, DEG)
    pi = order_tables(inverse_legendre, first)
    pi = pi.transpose(0, 2, 1, 3).reshape(2, 768, DEG)
    cube = filter_weight.reshape(16, 2, C, C)
    upper = jnp.concatenate([cube[:, 0], cube[:, 1]], axis=2)
    lower = jnp.concatenate([-cube[:, 1], cube[:, 0]], axis=2)
    kernel = jnp.concatenate([upper, lower], axis=1)

    cot = cotangent.reshape(1080, LON)
    cot, got[0] = fence(cot, got[0])
    wire_g = over_all(dft_g(cot, bdt))
    wire_g, kernel, pf, pi, got[1], got[2] = fence(wire_g, kernel, pf, pi, got[1], got[2])
    modes_g = leg_g(wire_g, pi)
    modes_g, got[3], got[4] = fence(modes_g, got[3], got[4])
    coef_g = over_polar(modes_g.reshape(16, 16, 768))
    coef_g, got[5] = fence(coef_g, got[5])
    mixed_g = mix(coef_g, kernel, True)
    mixed_g, got[0] = fence(mixed_g, got[0])
    mixed_g = over_polar(mixed_g).reshape(DEG, 768)
    wire_f = over_all(dft_f(me, got, bpt))

    back_g = over_all(syn_g(mixed_g, pf))
    modes_f = leg_f(wire_f, pf)
    modes_f, back_g = fence(modes_f, back_g)
    coef_f = over_polar(modes_f.reshape(16, 16, 768))

    pieces = list(idft_g(me, back_g, bp))
    pieces[0], coef_f = fence(pieces[0], coef_f)
    mixed_f = over_polar(mix(coef_f, kernel, False)).reshape(DEG, 768)
    got = hops(pieces, ORDER_E)
    mixed_f, got[1], got[2], got[3], got[4] = fence(mixed_f, got[1], got[2], got[3], got[4])
    back_f = over_all(syn_f(mixed_f, pi))
    filtered = idft_f(back_f, bdt)
    filtered, got[0] = fence(filtered, got[0])
    return filtered.reshape(ROWS, 24, LON), post(me, got)


def solution(mesh):
    return jax.shard_map(
        on_device,
        mesh=mesh,
        in_specs=(
            P("polar", "azimuth"),
            P("polar", "azimuth", None),
            P(None, "polar", None),
            P(None, "polar", None),
            P("polar", None),
        ),
        out_specs=(P("polar", "azimuth", None), P("polar", "azimuth")),
        check_vma=False,
    )
```

profile of v0, /device:TPU:1, one launch (start us, length us, event | category | flops | bytes accessed | tf_op | source)
XLA Modules:
  0.0 262.8 jit_solution(15563100206326457655)
XLA Ops:
  0.6 6.7 %prep.1 = (bf16[96,2304]{1,0:T(8,128)(2,1)}, bf16[96,2304]{1,0:T(8,128)(2,1)}, bf16[96,2304]{1,0:T(8,128)(2,1)}, bf16[96,2304]{1,0:T(8,128)(2,1)}, bf16[96,2304]...) custom-call(s32[1]{0:T(128)} %bitcast.me_ref, ...), custom_call_target="tpu_custom_call" | custom-call | tf_op jit(solution)/shard_map/prep/pallas_call | solution.py:76
  17.2 5.7 %dft_g.1 = bf16[128,4,1152]{2,1,0:T(4,128)(2,1)} custom-call(bf16[1080,1440]{1,0:T(8,128)(2,1)} %bitcast.35, bf16[512,1440]{1,0:T(8,128)(2,1)} %constant.18.clone.b_ref), custom_call_target="tpu_custom_call" | custom-call | tf_op jit(solution)/shard_map/dft_g/pallas_call | solution.py:123
  22.9 9.5 %all-to-all-start = ((bf16[128,4,1152]{2,1,0:T(4,128)(2,1)}), bf16[128,4,1152]{2,1,0:T(4,128)(2,1)}, u32[]{:S(2)}, u32[]{:S(2)}) async-start(bf16[128,4,1152]{2,1,0:T(4,128)(2,1)} %dft_g.1), calls=%async_computation | async-start | bytes 2359296 | tf_op jit(solution)/shard_map/all_to_all | solution.py:304
  32.4 5.1 %constant_dynamic-slice_fusion = (bf16[720,2,256]{2,1,0:T(2,128)(2,1)}, bf16[720,2,256]{2,1,0:T(2,128)(2,1)S(1)}) fusion(bf16[720,16,256]{2,1,0:T(8,128)(2,1)} %param.11, s32[]{:T(128)S(6)} %select_n.4, bf16[720,16,256]{2,1,0:T(8,128)(2,1)} %param.10), kind=kLoop, calls=%fused_computation.5 | loop fusion | bytes 2949124 | tf_op jit(solution)/shard_map/dynamic_slice | solution.py:281
  38.7 4.8 %reshape.41 = bf16[16,2,192,192]{3,2,1,0:T(8,128)(2,1)S(1)} reshape(bf16[16,73728]{1,0:T(8,128)(2,1)} %param.12) | data formatting | bytes 4718592 | tf_op jit(solution)/shard_map/reshape | solution.py:316
  43.8 4.3 %maximum_maximum_fusion.k_ref = bf16[16,384,384]{2,1,0:T(8,128)(2,1)} fusion(bf16[16,192,192]{2,1,0:T(8,128)(2,1)S(1)} %get-tuple-element.87, bf16[16,192,192]{2,1,0:T(8,128)(2,1)S(1)} %fusion, bf16[16,192,192]{2,1,0:T(8,128)(2,1)S(1)} %get-tuple-element.86), kind=kLoop, calls=%fused_computation | loop fusion | flops 18874368 | bytes 8257536 | tf_op jit(solution)/shard_map/concatenate | solution.py:319
  50.3 16.3 %all-to-all-done.r_ref = bf16[128,4,1152]{2,1,0:T(4,128)(2,1)} async-done(((bf16[128,4,1152]{2,1,0:T(4,128)(2,1)}), bf16[128,4,1152]{2,1,0:T(4,128)(2,1)}, u32[]{:S(2)}, u32[]{:S(2)}) %all-to-all-start) | async-done | bytes 1179680 | tf_op jit(solution)/shard_map/all_to_all | solution.py:304
  66.6 6.5 %leg_g.1 = bf16[256,768]{1,0:T(8,128)(2,1)} custom-call(bf16[128,4,1152]{2,1,0:T(4,128)(2,1)} %all-to-all-done.r_ref, bf16[2,768,256]{2,1,0:T(8,128)(2,1)} %bitcast.31), custom_call_target="tpu_custom_call" | custom-call | tf_op jit(solution)/shard_map/leg_g/pallas_call | solution.py:123
  73.1 5.8 %all-to-all-start.1 = ((bf16[16,16,768]{2,1,0:T(8,128)(2,1)}), bf16[16,16,768]{2,1,0:T(8,128)(2,1)S(1)}, u32[]{:S(2)}, u32[]{:S(2)}) async-start(bf16[16,16,768]{2,1,0:T(8,128)(2,1)} %bitcast.41), calls=%async_computation.1 | async-start | bytes 786432 | tf_op jit(solution)/shard_map/all_to_all | solution.py:307
  79.8 9.1 %all-to-all-done.1.r_ref = bf16[16,16,768]{2,1,0:T(8,128)(2,1)S(1)} async-done(((bf16[16,16,768]{2,1,0:T(8,128)(2,1)}), bf16[16,16,768]{2,1,0:T(8,128)(2,1)S(1)}, u32[]{:S(2)}, u32[]{:S(2)}) %all-to-all-start.1) | async-done | bytes 393248 | tf_op jit(solution)/shard_map/all_to_all | solution.py:307
  89.6 5.1 %mix_g.1 = bf16[16,16,768]{2,1,0:T(8,128)(2,1)} custom-call(bf16[16,16,768]{2,1,0:T(8,128)(2,1)} %copy-done.7, bf16[16,384,384]{2,1,0:T(8,128)(2,1)} %maximum_maximum_fusion.k_ref), custom_call_target="tpu_custom_call" | custom-call | tf_op jit(solution)/shard_map/mix_g/pallas_call | solution.py:123
  94.7 5.0 %all-to-all-start.3 = ((bf16[16,16,768]{2,1,0:T(8,128)(2,1)}), bf16[16,16,768]{2,1,0:T(8,128)(2,1)S(1)}, u32[]{:S(2)}, u32[]{:S(2)}) async-start(bf16[16,16,768]{2,1,0:T(8,128)(2,1)} %mix_g.1), calls=%async_computation.3 | async-start | bytes 786432 | tf_op jit(solution)/shard_map/all_to_all | solution.py:307
  101.2 6.7 %dft_f.1 = bf16[128,4,1152]{2,1,0:T(4,128)(2,1)} custom-call(s32[1]{0:T(128)} %bitcast.me_ref, bf16[96,2304]{1,0:T(8,128)(2,1)} %get-tuple-element.57.refs_0_, bf16[96,2304]{1,0:T(8,128)(2,1)} %collective-permute-done.refs_1_, bf16[96,2304]{1,0:T(8,128)(2,1)} %collective-permute-done.1.refs_2_, bf16[96,2304]{1,0:T(8,128)(2,1)} %collective-permute-done.2.refs_3_, ...), custom_call_target="tpu_custom_call" | custom-call | tf_op jit(solution)/shard_map/dft_f/pallas_call | solution.py:150
  109.6 5.4 %all-to-all-start.2 = ((bf16[128,4,1152]{2,1,0:T(4,128)(2,1)}), bf16[128,4,1152]{2,1,0:T(4,128)(2,1)S(1)}, u32[]{:S(2)}, u32[]{:S(2)}) async-start(bf16[128,4,1152]{2,1,0:T(4,128)(2,1)} %dft_f.1), calls=%async_computation.2 | async-start | bytes 2359296 | tf_op jit(solution)/shard_map/all_to_all | solution.py:304
  115.1 3.7 %syn_g.1 = bf16[128,4,1152]{2,1,0:T(4,128)(2,1)} custom-call(bf16[256,768]{1,0:T(8,128)(2,1)} %bitcast.40, bf16[2,768,256]{2,1,0:T(8,128)(2,1)} %bitcast.33), custom_call_target="tpu_custom_call" | custom-call | tf_op jit(solution)/shard_map/syn_g/pallas_call | solution.py:123
  118.8 16.5 %all-to-all-done.2.r_ref = bf16[128,4,1152]{2,1,0:T(4,128)(2,1)S(1)} async-done(((bf16[128,4,1152]{2,1,0:T(4,128)(2,1)}), bf16[128,4,1152]{2,1,0:T(4,128)(2,1)S(1)}, u32[]{:S(2)}, u32[]{:S(2)}) %all-to-all-start.2) | async-done | bytes 1179680 | tf_op jit(solution)/shard_map/all_to_all | solution.py:304
  135.4 4.8 %all-to-all-start.4 = ((bf16[128,4,1152]{2,1,0:T(4,128)(2,1)}), bf16[128,4,1152]{2,1,0:T(4,128)(2,1)S(1)}, u32[]{:S(2)}, u32[]{:S(2)}) async-start(bf16[128,4,1152]{2,1,0:T(4,128)(2,1)} %syn_g.1), calls=%async_computation.4 | async-start | bytes 2359296 | tf_op jit(solution)/shard_map/all_to_all | solution.py:304
  140.2 4.9 %leg_f.1 = bf16[256,768]{1,0:T(8,128)(2,1)} custom-call(bf16[128,4,1152]{2,1,0:T(4,128)(2,1)} %copy-done.1, bf16[2,768,256]{2,1,0:T(8,128)(2,1)} %bitcast.34), custom_call_target="tpu_custom_call" | custom-call | tf_op jit(solution)/shard_map/leg_f/pallas_call | solution.py:123
  145.1 15.5 %all-to-all-done.4.y_ref = bf16[128,4,1152]{2,1,0:T(4,128)(2,1)S(1)} async-done(((bf16[128,4,1152]{2,1,0:T(4,128)(2,1)}), bf16[128,4,1152]{2,1,0:T(4,128)(2,1)S(1)}, u32[]{:S(2)}, u32[]{:S(2)}) %all-to-all-start.4) | async-done | bytes 1179680 | tf_op jit(solution)/shard_map/all_to_all | solution.py:304
  160.6 4.7 %all-to-all-start.5 = ((bf16[16,16,768]{2,1,0:T(8,128)(2,1)}), bf16[16,16,768]{2,1,0:T(8,128)(2,1)S(1)}, u32[]{:S(2)}, u32[]{:S(2)}) async-start(bf16[16,16,768]{2,1,0:T(8,128)(2,1)} %bitcast.39), calls=%async_computation.5 | async-start | bytes 786432 | tf_op jit(solution)/shard_map/all_to_all | solution.py:307
  165.3 6.3 %idft_g.1 = (bf16[96,2304]{1,0:T(8,128)(2,1)}, bf16[96,2304]{1,0:T(8,128)(2,1)}, bf16[96,2304]{1,0:T(8,128)(2,1)}, bf16[96,2304]{1,0:T(8,128)(2,1)}, bf16[96,230...) custom-call(s32[1]{0:T(128)} %bitcast.me_ref, ...), custom_call_target="tpu_custom_call" | custom-call | tf_op jit(solution)/shard_map/idft_g/pallas_call | solution.py:269
  176.9 4.5 %mix_f.1 = bf16[16,16,768]{2,1,0:T(8,128)(2,1)} custom-call(bf16[16,16,768]{2,1,0:T(8,128)(2,1)} %copy-done.6, bf16[16,384,384]{2,1,0:T(8,128)(2,1)} %maximum_maximum_fusion.k_ref), custom_call_target="tpu_custom_call" | custom-call | tf_op jit(solution)/shard_map/mix_f/pallas_call | solution.py:123
  181.4 8.2 %all-to-all-start.6 = ((bf16[16,16,768]{2,1,0:T(8,128)(2,1)}), bf16[16,16,768]{2,1,0:T(8,128)(2,1)S(1)}, u32[]{:S(2)}, u32[]{:S(2)}) async-start(bf16[16,16,768]{2,1,0:T(8,128)(2,1)} %mix_f.1), calls=%async_computation.6 | async-start | bytes 786432 | tf_op jit(solution)/shard_map/all_to_all | solution.py:307
  189.6 5.7 %collective-permute-done.8.refs_2_ = bf16[96,2304]{1,0:T(8,128)(2,1)S(1)} collective-permute-done((bf16[96,2304]{1,0:T(8,128)(2,1)}, bf16[96,2304]{1,0:T(8,128)(2,1)S(1)}, u32[]{:S(2)}, u32[]{:S(2)}) %collective-permute-start.8) | collective-permute-done | bytes 442400 | tf_op jit(solution)/shard_map/ppermute | solution.py:288
  195.3 9.9 %collective-permute-done.10.refs_4_ = bf16[96,2304]{1,0:T(8,128)(2,1)S(1)} collective-permute-done((bf16[96,2304]{1,0:T(8,128)(2,1)}, bf16[96,2304]{1,0:T(8,128)(2,1)S(1)}, u32[]{:S(2)}, u32[]{:S(2)}) %collective-permute-start.10) | collective-permute-done | bytes 442400 | tf_op jit(solution)/shard_map/ppermute | solution.py:288
  205.9 6.0 %syn_f.1 = bf16[128,4,1152]{2,1,0:T(4,128)(2,1)} custom-call(bf16[256,768]{1,0:T(8,128)(2,1)} %bitcast.42, bf16[2,768,256]{2,1,0:T(8,128)(2,1)} %bitcast.32), custom_call_target="tpu_custom_call" | custom-call | tf_op jit(solution)/shard_map/syn_f/pallas_call | solution.py:123
  212.0 7.0 %all-to-all-start.7 = ((bf16[128,4,1152]{2,1,0:T(4,128)(2,1)}), bf16[128,4,1152]{2,1,0:T(4,128)(2,1)S(1)}, u32[]{:S(2)}, u32[]{:S(2)}) async-start(bf16[128,4,1152]{2,1,0:T(4,128)(2,1)} %syn_f.1), calls=%async_computation.7 | async-start | bytes 2359296 | tf_op jit(solution)/shard_map/all_to_all | solution.py:304
  221.7 2.9 %collective-permute-start.13 = (bf16[96,2304]{1,0:T(8,128)(2,1)}, bf16[96,2304]{1,0:T(8,128)(2,1)}, u32[]{:S(2)}, u32[]{:S(2)}) collective-permute-start(bf16[96,2304]{1,0:T(8,128)(2,1)} %get-tuple-element.85), channel_id=1, source_target_pairs={{0,2},{1,3},{2,0},{3,1},{4,6},{5,7},{6,4},{7,5},{8,10},{9,11},{10,... | collective-permute-start | bytes 1327112 | tf_op jit(solution)/shard_map/ppermute | solution.py:288
  224.7 14.6 %all-to-all-done.7.y_ref = bf16[128,4,1152]{2,1,0:T(4,128)(2,1)S(1)} async-done(((bf16[128,4,1152]{2,1,0:T(4,128)(2,1)}), bf16[128,4,1152]{2,1,0:T(4,128)(2,1)S(1)}, u32[]{:S(2)}, u32[]{:S(2)}) %all-to-all-start.7) | async-done | bytes 1179680 | tf_op jit(solution)/shard_map/all_to_all | solution.py:304
  240.3 5.4 %idft_f.1 = bf16[1080,1440]{1,0:T(8,128)(2,1)} custom-call(bf16[128,4,1152]{2,1,0:T(4,128)(2,1)} %copy-done.2, bf16[512,1440]{1,0:T(8,128)(2,1)} %constant.18.clone.b_ref), custom_call_target="tpu_custom_call" | custom-call | tf_op jit(solution)/shard_map/idft_f/pallas_call | solution.py:123
  245.7 8.3 %collective-permute-done.12.refs_6_ = bf16[96,2304]{1,0:T(8,128)(2,1)} collective-permute-done((bf16[96,2304]{1,0:T(8,128)(2,1)}, bf16[96,2304]{1,0:T(8,128)(2,1)}, u32[]{:S(2)}, u32[]{:S(2)}) %collective-permute-start.12) | collective-permute-done | bytes 442400 | tf_op jit(solution)/shard_map/ppermute | solution.py:288
  255.8 6.6 %post.1 = bf16[45,34560]{1,0:T(8,128)(2,1)} custom-call(s32[1]{0:T(128)} %bitcast.me_ref, bf16[96,2304]{1,0:T(8,128)(2,1)} %get-tuple-element.78.refs_0_, bf16[96,2304]{1,0:T(8,128)(2,1)} %copy-done.10, bf16[96,2304]{1,0:T(8,128)(2,1)} %copy-done.11, bf16[96,2304]{1,0:T(8,128)(2,1)} %copy-done.12, bf16[96,2304]{1,0:T(8,128)(2,1)} %copy-done.13, ...), custom_call_target="tpu_custom_call" | custom-call | tf_op jit(solution)/shard_map/post/pallas_call | solution.py:107
  (66 shorter events, 30.1 us)
Async XLA Ops:
  7.4 42.9 %collective-permute-start = (bf16[96,2304]{1,0:T(8,128)(2,1)}, bf16[96,2304]{1,0:T(8,128)(2,1)}, u32[]{:S(2)}, u32[]{:S(2)}) collective-permute-start(bf16[96,2304]{1,0:T(8,128)(2,1)} %get-tuple-element.46), channel_id=1, source_target_pairs={{0,1},{1,0},{2,3},{3,2},{4,5},{5,4},{6,7},{7,6},{8,9},{9,8},{10,11... | collective-permute-start | bytes 1327112 | tf_op jit(solution)/shard_map/ppermute | solution.py:288
  9.9 40.4 %collective-permute-start.1 = (bf16[96,2304]{1,0:T(8,128)(2,1)}, bf16[96,2304]{1,0:T(8,128)(2,1)}, u32[]{:S(2)}, u32[]{:S(2)}) collective-permute-start(bf16[96,2304]{1,0:T(8,128)(2,1)} %get-tuple-element.47), channel_id=1, source_target_pairs={{0,3},{1,2},{2,1},{3,0},{4,7},{5,6},{6,5},{7,4},{8,11},{9,10},{10,... | collective-permute-start | bytes 1327112 | tf_op jit(solution)/shard_map/ppermute | solution.py:288
  12.1 61.0 %collective-permute-start.2 = (bf16[96,2304]{1,0:T(8,128)(2,1)}, bf16[96,2304]{1,0:T(8,128)(2,1)}, u32[]{:S(2)}, u32[]{:S(2)}) collective-permute-start(bf16[96,2304]{1,0:T(8,128)(2,1)} %get-tuple-element.50), channel_id=1, source_target_pairs={{0,7},{1,6},{2,5},{3,4},{4,3},{5,2},{6,1},{7,0},{8,15},{9,14},{10,... | collective-permute-start | bytes 1327112 | tf_op jit(solution)/shard_map/ppermute | solution.py:288
  13.5 59.6 %collective-permute-start.3 = (bf16[96,2304]{1,0:T(8,128)(2,1)}, bf16[96,2304]{1,0:T(8,128)(2,1)}, u32[]{:S(2)}, u32[]{:S(2)}) collective-permute-start(bf16[96,2304]{1,0:T(8,128)(2,1)} %get-tuple-element.51), channel_id=1, source_target_pairs={{0,6},{1,7},{2,4},{3,5},{4,2},{5,3},{6,0},{7,1},{8,14},{9,15},{10,... | collective-permute-start | bytes 1327112 | tf_op jit(solution)/shard_map/ppermute | solution.py:288
  15.5 64.2 %collective-permute-start.4 = (bf16[96,2304]{1,0:T(8,128)(2,1)}, bf16[96,2304]{1,0:T(8,128)(2,1)}, u32[]{:S(2)}, u32[]{:S(2)}) collective-permute-start(bf16[96,2304]{1,0:T(8,128)(2,1)} %get-tuple-element.53), channel_id=1, source_target_pairs={{0,5},{1,4},{2,7},{3,6},{4,1},{5,0},{6,3},{7,2},{8,13},{9,12},{10,... | collective-permute-start | bytes 1327112 | tf_op jit(solution)/shard_map/ppermute | solution.py:288
  22.9 43.7 %all-to-all-start = ((bf16[128,4,1152]{2,1,0:T(4,128)(2,1)}), bf16[128,4,1152]{2,1,0:T(4,128)(2,1)}, u32[]{:S(2)}, u32[]{:S(2)}) async-start(bf16[128,4,1152]{2,1,0:T(4,128)(2,1)} %dft_g.1), calls=%async_computation | async-start | bytes 2359296 | tf_op jit(solution)/shard_map/all_to_all | solution.py:304
  43.8 4.3 %copy-start.3 = (bf16[720,2,256]{2,1,0:T(2,128)(2,1)S(1)}, bf16[720,2,256]{2,1,0:T(2,128)(2,1)}, u32[]{:S(2)}) copy-start(bf16[720,2,256]{2,1,0:T(2,128)(2,1)} %get-tuple-element.88) | copy-start | bytes 2211844
  48.1 30.8 %copy-start.15 = (bf16[96,2304]{1,0:T(8,128)(2,1)S(1)}, bf16[96,2304]{1,0:T(8,128)(2,1)}, u32[]{:S(2)}) copy-start(bf16[96,2304]{1,0:T(8,128)(2,1)} %get-tuple-element.63) | copy-start | bytes 1327108
  48.1 30.8 %copy-start.14 = (bf16[96,2304]{1,0:T(8,128)(2,1)S(1)}, bf16[96,2304]{1,0:T(8,128)(2,1)}, u32[]{:S(2)}) copy-start(bf16[96,2304]{1,0:T(8,128)(2,1)} %get-tuple-element.64) | copy-start | bytes 1327108
  73.1 15.7 %all-to-all-start.1 = ((bf16[16,16,768]{2,1,0:T(8,128)(2,1)}), bf16[16,16,768]{2,1,0:T(8,128)(2,1)S(1)}, u32[]{:S(2)}, u32[]{:S(2)}) async-start(bf16[16,16,768]{2,1,0:T(8,128)(2,1)} %bitcast.41), calls=%async_computation.1 | async-start | bytes 786432 | tf_op jit(solution)/shard_map/all_to_all | solution.py:307
  78.9 20.8 %collective-permute-start.5 = (bf16[96,2304]{1,0:T(8,128)(2,1)S(1)}, bf16[96,2304]{1,0:T(8,128)(2,1)S(1)}, u32[]{:S(2)}, u32[]{:S(2)}) collective-permute-start(bf16[96,2304]{1,0:T(8,128)(2,1)S(1)} %copy-done.15), channel_id=1, source_target_pairs={{0,4},{1,5},{2,6},{3,7},{4,0},{5,1},{6,2},{7,3},{8,12},{9,13},{10,... | collective-permute-start | bytes 1327112 | tf_op jit(solution)/shard_map/ppermute | solution.py:288
  79.0 20.7 %collective-permute-start.6 = (bf16[96,2304]{1,0:T(8,128)(2,1)S(1)}, bf16[96,2304]{1,0:T(8,128)(2,1)S(1)}, u32[]{:S(2)}, u32[]{:S(2)}) collective-permute-start(bf16[96,2304]{1,0:T(8,128)(2,1)S(1)} %copy-done.14), channel_id=1, source_target_pairs={{0,2},{1,3},{2,0},{3,1},{4,6},{5,7},{6,4},{7,5},{8,10},{9,11},{10,... | collective-permute-start | bytes 1327112 | tf_op jit(solution)/shard_map/ppermute | solution.py:288
  94.7 15.0 %all-to-all-start.3 = ((bf16[16,16,768]{2,1,0:T(8,128)(2,1)}), bf16[16,16,768]{2,1,0:T(8,128)(2,1)S(1)}, u32[]{:S(2)}, u32[]{:S(2)}) async-start(bf16[16,16,768]{2,1,0:T(8,128)(2,1)} %mix_g.1), calls=%async_computation.3 | async-start | bytes 786432 | tf_op jit(solution)/shard_map/all_to_all | solution.py:307
  109.6 5.5 %copy-start.4 = (bf16[16,16,768]{2,1,0:T(8,128)(2,1)}, bf16[16,16,768]{2,1,0:T(8,128)(2,1)S(1)}, u32[]{:S(2)}) copy-start(bf16[16,16,768]{2,1,0:T(8,128)(2,1)S(1)} %all-to-all-done.3) | copy-start | bytes 1179652
  109.6 25.7 %all-to-all-start.2 = ((bf16[128,4,1152]{2,1,0:T(4,128)(2,1)}), bf16[128,4,1152]{2,1,0:T(4,128)(2,1)S(1)}, u32[]{:S(2)}, u32[]{:S(2)}) async-start(bf16[128,4,1152]{2,1,0:T(4,128)(2,1)} %dft_f.1), calls=%async_computation.2 | async-start | bytes 2359296 | tf_op jit(solution)/shard_map/all_to_all | solution.py:304
  135.4 4.8 %copy-start.1 = (bf16[128,4,1152]{2,1,0:T(4,128)(2,1)}, bf16[128,4,1152]{2,1,0:T(4,128)(2,1)S(1)}, u32[]{:S(2)}) copy-start(bf16[128,4,1152]{2,1,0:T(4,128)(2,1)S(1)} %all-to-all-done.2.r_ref) | copy-start | bytes 3538948
  135.4 25.2 %all-to-all-start.4 = ((bf16[128,4,1152]{2,1,0:T(4,128)(2,1)}), bf16[128,4,1152]{2,1,0:T(4,128)(2,1)S(1)}, u32[]{:S(2)}, u32[]{:S(2)}) async-start(bf16[128,4,1152]{2,1,0:T(4,128)(2,1)} %syn_g.1), calls=%async_computation.4 | async-start | bytes 2359296 | tf_op jit(solution)/shard_map/all_to_all | solution.py:304
  160.6 4.7 %copy-start = (bf16[128,4,1152]{2,1,0:T(4,128)(2,1)}, bf16[128,4,1152]{2,1,0:T(4,128)(2,1)S(1)}, u32[]{:S(2)}) copy-start(bf16[128,4,1152]{2,1,0:T(4,128)(2,1)S(1)} %all-to-all-done.4.y_ref) | copy-start | bytes 3538948
  160.6 15.6 %all-to-all-start.5 = ((bf16[16,16,768]{2,1,0:T(8,128)(2,1)}), bf16[16,16,768]{2,1,0:T(8,128)(2,1)S(1)}, u32[]{:S(2)}, u32[]{:S(2)}) async-start(bf16[16,16,768]{2,1,0:T(8,128)(2,1)} %bitcast.39), calls=%async_computation.5 | async-start | bytes 786432 | tf_op jit(solution)/shard_map/all_to_all | solution.py:307
  171.5 18.1 %collective-permute-start.7 = (bf16[96,2304]{1,0:T(8,128)(2,1)}, bf16[96,2304]{1,0:T(8,128)(2,1)S(1)}, u32[]{:S(2)}, u32[]{:S(2)}) collective-permute-start(bf16[96,2304]{1,0:T(8,128)(2,1)} %get-tuple-element.71), channel_id=1, source_target_pairs={{0,7},{1,6},{2,5},{3,4},{4,3},{5,2},{6,1},{7,0},{8,15},{9,14},{10,... | collective-permute-start | bytes 1327112 | tf_op jit(solution)/shard_map/ppermute | solution.py:288
  172.3 23.0 %collective-permute-start.8 = (bf16[96,2304]{1,0:T(8,128)(2,1)}, bf16[96,2304]{1,0:T(8,128)(2,1)S(1)}, u32[]{:S(2)}, u32[]{:S(2)}) collective-permute-start(bf16[96,2304]{1,0:T(8,128)(2,1)} %get-tuple-element.72), channel_id=1, source_target_pairs={{0,6},{1,7},{2,4},{3,5},{4,2},{5,3},{6,0},{7,1},{8,14},{9,15},{10,... | collective-permute-start | bytes 1327112 | tf_op jit(solution)/shard_map/ppermute | solution.py:288
  174.4 20.9 %collective-permute-start.9 = (bf16[96,2304]{1,0:T(8,128)(2,1)}, bf16[96,2304]{1,0:T(8,128)(2,1)S(1)}, u32[]{:S(2)}, u32[]{:S(2)}) collective-permute-start(bf16[96,2304]{1,0:T(8,128)(2,1)} %get-tuple-element.73), channel_id=1, source_target_pairs={{0,1},{1,0},{2,3},{3,2},{4,5},{5,4},{6,7},{7,6},{8,9},{9,8},{10,11... | collective-permute-start | bytes 1327112 | tf_op jit(solution)/shard_map/ppermute | solution.py:288
  175.9 29.2 %collective-permute-start.10 = (bf16[96,2304]{1,0:T(8,128)(2,1)}, bf16[96,2304]{1,0:T(8,128)(2,1)S(1)}, u32[]{:S(2)}, u32[]{:S(2)}) collective-permute-start(bf16[96,2304]{1,0:T(8,128)(2,1)} %get-tuple-element.74), channel_id=1, source_target_pairs={{0,3},{1,2},{2,1},{3,0},{4,7},{5,6},{6,5},{7,4},{8,11},{9,10},{10,... | collective-permute-start | bytes 1327112 | tf_op jit(solution)/shard_map/ppermute | solution.py:288
  181.4 23.8 %all-to-all-start.6 = ((bf16[16,16,768]{2,1,0:T(8,128)(2,1)}), bf16[16,16,768]{2,1,0:T(8,128)(2,1)S(1)}, u32[]{:S(2)}, u32[]{:S(2)}) async-start(bf16[16,16,768]{2,1,0:T(8,128)(2,1)} %mix_f.1), calls=%async_computation.6 | async-start | bytes 786432 | tf_op jit(solution)/shard_map/all_to_all | solution.py:307
  189.6 66.2 %copy-start.10 = (bf16[96,2304]{1,0:T(8,128)(2,1)}, bf16[96,2304]{1,0:T(8,128)(2,1)S(1)}, u32[]{:S(2)}) copy-start(bf16[96,2304]{1,0:T(8,128)(2,1)S(1)} %collective-permute-done.7.refs_1_) | copy-start | bytes 1327108
  195.3 60.5 %copy-start.11 = (bf16[96,2304]{1,0:T(8,128)(2,1)}, bf16[96,2304]{1,0:T(8,128)(2,1)S(1)}, u32[]{:S(2)}) copy-start(bf16[96,2304]{1,0:T(8,128)(2,1)S(1)} %collective-permute-done.8.refs_2_) | copy-start | bytes 1327108
  195.3 60.5 %copy-start.12 = (bf16[96,2304]{1,0:T(8,128)(2,1)}, bf16[96,2304]{1,0:T(8,128)(2,1)S(1)}, u32[]{:S(2)}) copy-start(bf16[96,2304]{1,0:T(8,128)(2,1)S(1)} %collective-permute-done.9.refs_3_) | copy-start | bytes 1327108
  205.1 50.6 %copy-start.13 = (bf16[96,2304]{1,0:T(8,128)(2,1)}, bf16[96,2304]{1,0:T(8,128)(2,1)S(1)}, u32[]{:S(2)}) copy-start(bf16[96,2304]{1,0:T(8,128)(2,1)S(1)} %collective-permute-done.10.refs_4_) | copy-start | bytes 1327108
  212.0 27.3 %all-to-all-start.7 = ((bf16[128,4,1152]{2,1,0:T(4,128)(2,1)}), bf16[128,4,1152]{2,1,0:T(4,128)(2,1)S(1)}, u32[]{:S(2)}, u32[]{:S(2)}) async-start(bf16[128,4,1152]{2,1,0:T(4,128)(2,1)} %syn_f.1), calls=%async_computation.7 | async-start | bytes 2359296 | tf_op jit(solution)/shard_map/all_to_all | solution.py:304
  219.0 26.7 %collective-permute-start.11 = (bf16[96,2304]{1,0:T(8,128)(2,1)}, bf16[96,2304]{1,0:T(8,128)(2,1)}, u32[]{:S(2)}, u32[]{:S(2)}) collective-permute-start(bf16[96,2304]{1,0:T(8,128)(2,1)} %get-tuple-element.83), channel_id=1, source_target_pairs={{0,5},{1,4},{2,7},{3,6},{4,1},{5,0},{6,3},{7,2},{8,13},{9,12},{10,... | collective-permute-start | bytes 1327112 | tf_op jit(solution)/shard_map/ppermute | solution.py:288
  221.5 32.5 %collective-permute-start.12 = (bf16[96,2304]{1,0:T(8,128)(2,1)}, bf16[96,2304]{1,0:T(8,128)(2,1)}, u32[]{:S(2)}, u32[]{:S(2)}) collective-permute-start(bf16[96,2304]{1,0:T(8,128)(2,1)} %get-tuple-element.84), channel_id=1, source_target_pairs={{0,4},{1,5},{2,6},{3,7},{4,0},{5,1},{6,2},{7,3},{8,12},{9,13},{10,... | collective-permute-start | bytes 1327112 | tf_op jit(solution)/shard_map/ppermute | solution.py:288
  221.7 34.0 %collective-permute-start.13 = (bf16[96,2304]{1,0:T(8,128)(2,1)}, bf16[96,2304]{1,0:T(8,128)(2,1)}, u32[]{:S(2)}, u32[]{:S(2)}) collective-permute-start(bf16[96,2304]{1,0:T(8,128)(2,1)} %get-tuple-element.85), channel_id=1, source_target_pairs={{0,2},{1,3},{2,0},{3,1},{4,6},{5,7},{6,4},{7,5},{8,10},{9,11},{10,... | collective-permute-start | bytes 1327112 | tf_op jit(solution)/shard_map/ppermute | solution.py:288
  (6 other events, 4.9 us)
where the time goes:
time: 267 us; the launch traced here: 263 us
  waiting for transfers between devices  99.2 us (37%)
  starting transfers between devices  71.5 us (27%)
  Pallas kernels  68.1 us (26%)
  local copies, waits for them, and re-layouts  18.3 us (7%)
  other arithmetic  4.41 us (2%)
    all_to_all x4, waiting for transfers between devices, over_all(): return lax.all_to_all(x, both, 0, 0)  62.9 us
    pallas_call x8, Pallas kernels, whole(): pl.pallas_call(body, out_shape=jax.ShapeDtypeStruct(out, BF), scratch_sha...  41.8 us
    all_to_all x4, starting transfers between devices, over_all(): return lax.all_to_all(x, both, 0, 0)  26.8 us
    ppermute x14, waiting for transfers between devices, hop(): return lax.ppermute(piece, 'azimuth', [(a, a ^ s) for a in range(NA)])  25.6 us
    all_to_all x4, starting transfers between devices, over_polar(): return lax.all_to_all(x, 'polar', 0, 0)  23.6 us
    ppermute x14, starting transfers between devices, hop(): return lax.ppermute(piece, 'azimuth', [(a, a ^ s) for a in range(NA)])  21 us
    all_to_all x4, waiting for transfers between devices, over_polar(): return lax.all_to_all(x, 'polar', 0, 0)  10.7 us
    pallas_call x1, Pallas kernels, prep(): pl.pallas_call(prep_body, grid_spec=pltpu.PrefetchScalarGridSpec(num_scal...  6.74 us
  transfers between devices with their start and end apart: 22, of which 10 were waited for; matrix products, arithmetic and copies ran while one was open for 7% of the time, Pallas kernels for 19%

commit v1 on v0

--- a/solution.py
+++ b/solution.py
@@ -14,8 +14,8 @@
 C = 192
 DEG = 256
 ORD = 256
-ORDER_A = (0, 1, 3, 7, 6, 5, 4, 2)
-ORDER_E = (0, 7, 6, 1, 3, 5, 4, 2)
+ORDER = (0, 7, 6, 5, 4, 2, 3, 1)
+ORDER_E = (0, 2, 3, 1, 7, 6, 5, 4)
 NP = 16
 NA = 8
 ROWS = 45
@@ -67,7 +67,7 @@
             for t in range(3):
                 s_ref[3 * k + t, pl.ds(lp, 8, stride=16), :] = v[:, (3 * lp + t) * 128:(3 * lp + t + 1) * 128]
     for s in range(NA):
-        row = pl.multiple_of(16 * (me ^ ORDER_A[s]), 16)
+        row = pl.multiple_of(16 * (me ^ ORDER[s]), 16)
         for q in range(18):
             outs[s][:, q * 128:(q + 1) * 128] = s_ref[q, pl.ds(row, 16), :].astype(BF)
 
@@ -130,31 +130,32 @@
 
 
 def dft_f_body(me_ref, *refs):
-    r_refs, b_ref, o_ref, x_ref = refs[:8], refs[8], refs[9], refs[10]
+    r_refs, b_ref, g_ref, o_ref, x_ref = refs[:8], *refs[8:]
     me = me_ref[0]
     for s in range(NA):
-        row = pl.multiple_of(LP * (me ^ ORDER_A[s]), 32)
+        row = pl.multiple_of(LP * (me ^ ORDER[s]), 32)
         for k in range(SLOTS):
             v = r_refs[s][:, 384 * k:384 * k + 384]
             x_ref[pl.ds(row, LP), C * k:C * k + C] = v[:, :C]
             x_ref[pl.ds(768 + row, LP), C * k:C * k + C] = v[:, C:]
     y = dot(b_ref[...], x_ref[...], 1, 0).astype(BF)
-    o_ref[...] = y.reshape(128, 4, W)
+    o_ref[:, :4, :] = y.reshape(128, 4, W)
+    o_ref[:, 4:, :] = g_ref[...]
 
 
 SMEM = pl.BlockSpec(memory_space=pltpu.SMEM)
 VMEM = pl.BlockSpec(memory_space=pltpu.VMEM)
 
 
-def dft_f(me, pieces, bpt):
+def dft_f(me, pieces, bpt, wire_g):
     return pl.pallas_call(
         dft_f_body,
-        in_specs=[SMEM] + [VMEM] * 9,
-        out_shape=jax.ShapeDtypeStruct((128, 4, W), BF),
+        in_specs=[SMEM] + [VMEM] * 10,
+        out_shape=jax.ShapeDtypeStruct((128, 8, W), BF),
         scratch_shapes=[pltpu.VMEM((1536, W), BF)],
         compiler_params=params(),
         name="dft_f",
-    )(me, *pieces, bpt)
+    )(me, *pieces, bpt, wire_g)
 
 
 def dft_g_body(x_ref, b_ref, o_ref):
@@ -167,84 +168,66 @@
     return whole(dft_g_body, (128, 4, W), x, bdt, name="dft_g")
 
 
-def leg_f_body(r_ref, p_ref, o_ref, s_ref):
+def leg_body(r_ref, pf_ref, pi_ref, o_ref, s_ref, t_ref):
     for m in range(2):
         for r in range(2):
             v = r_ref[:, 2 * m + r, :]
             for k in range(SLOTS):
-                s_ref[128 * k:128 * k + 128, C * r:C * r + C] = v[:, C * k:C * k + C]
-        y = dot(p_ref[m], s_ref[...], 0, 0).astype(BF)
-        o_ref[:, 384 * m:384 * m + 384] = y
-
-
-def leg_f(r, pf):
-    return whole(leg_f_body, (DEG, 768), r, pf, scratch=[pltpu.VMEM((768, 384), BF)], name="leg_f")
-
-
-def leg_g_body(r_ref, p_ref, o_ref, s_ref):
-    for m in range(2):
-        for r in range(2):
-            v = r_ref[:, 2 * m + r, :].astype(F32).reshape(NP, NA, W)
+                s_ref[m, 128 * k:128 * k + 128, C * r:C * r + C] = v[:, C * k:C * k + C]
+            v = r_ref[:, 4 + 2 * m + r, :].astype(F32).reshape(NP, NA, W)
             for a in range(NA):
                 va = v[:, a, :].astype(BF)
                 for t in range(48):
-                    s_ref[16 * t:16 * t + 16, C * r + 24 * a:C * r + 24 * a + 24] = va[:, 24 * t:24 * t + 24]
-        y = dot(p_ref[m], s_ref[...], 0, 0).astype(BF)
-        o_ref[:, 384 * m:384 * m + 384] = y
-
-
-def leg_g(r, pi):
-    return whole(leg_g_body, (DEG, 768), r, pi, scratch=[pltpu.VMEM((768, 384), BF)], name="leg_g")
-
-
-def mix_body(adjoint, r_ref, k_ref, o_ref, s_ref):
+                    t_ref[m, 16 * t:16 * t + 16, C * r + 24 * a:C * r + 24 * a + 24] = va[:, 24 * t:24 * t + 24]
+        o_ref[:, 384 * m:384 * m + 384] = dot(pf_ref[m], s_ref[m], 0, 0).astype(BF)
+        o_ref[:, 768 + 384 * m:768 + 384 * m + 384] = dot(pi_ref[m], t_ref[m], 0, 0).astype(BF)
+
+
+def leg(r, pf, pi):
+    return whole(leg_body, (DEG, 1536), r, pf, pi, scratch=[pltpu.VMEM((2, 768, 384), BF)] * 2, name="leg")
+
+
+def mix_body(r_ref, k_ref, o_ref, s_ref):
     i = lax.broadcasted_iota(jnp.int32, (256, 256), 0)
     j = lax.broadcasted_iota(jnp.int32, (256, 256), 1)
     perm = ((i // 16 == j % 16) & (i % 16 == j // 16)).astype(F32).astype(BF)
-    x = dot(perm, r_ref[...].reshape(256, 768), 1, 0).astype(BF)
+    x = dot(perm, r_ref[...].reshape(256, 1536), 1, 0).astype(BF)
     for l in range(16):
-        v = x[16 * l:16 * l + 16]
-        v = jnp.concatenate([v[:, :384], v[:, 384:]], 0)
-        y = dot(v, k_ref[l], 1, 1 if adjoint else 0).astype(BF)
-        s_ref[16 * l:16 * l + 16, :384] = y[:16]
-        s_ref[16 * l:16 * l + 16, 384:] = y[16:]
-    o_ref[...] = dot(perm, s_ref[...], 1, 0).astype(BF).reshape(16, 16, 768)
-
-
-def mix(r, k, adjoint):
-    return whole(functools.partial(mix_body, adjoint), (16, 16, 768), r, k, scratch=[pltpu.VMEM((256, 768), BF)], name="mix_g" if adjoint else "mix_f")
-
-
-def syn_f_body(x_ref, p_ref, o_ref, z_ref):
+        for side in range(2):
+            v = x[16 * l:16 * l + 16, 768 * side:768 * side + 768]
+            v = jnp.concatenate([v[:, :384], v[:, 384:]], 0)
+            y = dot(v, k_ref[l], 1, side).astype(BF)
+            s_ref[16 * l:16 * l + 16, 768 * side:768 * side + 384] = y[:16]
+            s_ref[16 * l:16 * l + 16, 768 * side + 384:768 * side + 768] = y[16:]
+    o_ref[...] = dot(perm, s_ref[...], 1, 0).astype(BF).reshape(16, 16, 1536)
+
+
+def mix(r, k):
+    return whole(mix_body, (16, 16, 1536), r, k, scratch=[pltpu.VMEM((256, 1536), BF)], name="mix")
+
+
+def syn_body(x_ref, pf_ref, pi_ref, o_ref, z_ref, y_ref):
     for m in range(2):
-        y = dot(p_ref[m], x_ref[:, 384 * m:384 * m + 384], 1, 0).astype(BF)
+        y = dot(pi_ref[m], x_ref[:, 384 * m:384 * m + 384], 1, 0).astype(BF)
         for r in range(2):
             for a in range(NA):
                 for t in range(48):
                     z_ref[a, :, 24 * t:24 * t + 24] = y[16 * t:16 * t + 16, C * r + 24 * a:C * r + 24 * a + 24]
             for p in range(NP):
                 o_ref[8 * p:8 * p + 8, 2 * m + r, :] = z_ref[:, p, :]
-
-
-def syn_f(x, pi):
-    return whole(syn_f_body, (128, 4, W), x, pi, scratch=[pltpu.VMEM((8, 16, W), BF)], name="syn_f")
-
-
-def syn_g_body(x_ref, p_ref, o_ref, z_ref):
-    for m in range(2):
-        y = dot(p_ref[m], x_ref[:, 384 * m:384 * m + 384], 1, 0).astype(BF)
+        y = dot(pf_ref[m], x_ref[:, 768 + 384 * m:768 + 384 * m + 384], 1, 0).astype(BF)
         for r in range(2):
             for k in range(SLOTS):
-                z_ref[:, C * k:C * k + C] = y[128 * k:128 * k + 128, C * r:C * r + C]
-            o_ref[:, 2 * m + r, :] = z_ref[...]
-
-
-def syn_g(x, pf):
-    return whole(syn_g_body, (128, 4, W), x, pf, scratch=[pltpu.VMEM((128, W), BF)], name="syn_g")
+                y_ref[:, C * k:C * k + C] = y[128 * k:128 * k + 128, C * r:C * r + C]
+            o_ref[:, 4 + 2 * m + r, :] = y_ref[...]
+
+
+def syn(x, pf, pi):
+    return whole(syn_body, (128, 8, W), x, pf, pi, scratch=[pltpu.VMEM((8, 16, W), BF), pltpu.VMEM((128, W), BF)], name="syn")
 
 
 def idft_f_body(y_ref, b_ref, o_ref):
-    y = y_ref[...].reshape(512, W)
+    y = y_ref[:, :4, :].reshape(512, W)
     o_ref[...] = dot(y[:, :1080], b_ref[...], 0, 0).astype(BF)
 
 
@@ -255,7 +238,7 @@
 def idft_g_body(me_ref, y_ref, b_ref, *refs):
     outs, z_ref = refs[:8], refs[8]
     me = me_ref[0]
-    y = y_ref[...].reshape(512, W)
+    y = y_ref[:, 4:, :].reshape(512, W)
     z_ref[...] = dot(b_ref[...], y, 1, 0).astype(BF)
     for s in range(NA):
         row = pl.multiple_of(LP * (me ^ ORDER_E[s]), 32)
@@ -307,7 +290,7 @@
         return lax.all_to_all(x, "polar", 0, 0)
 
     pieces = list(prep(me, grid_input))
-    got = hops(pieces, ORDER_A)
+    got = hops(pieces, ORDER)
 
     pf = order_tables(forward_legendre, first)
     pf = pf.reshape(2, NP, SLOTS, NA, DEG).transpose(0, 2, 1, 3, 4).reshape(2, 768, DEG)
@@ -320,30 +303,15 @@
 
     cot = cotangent.reshape(1080, LON)
     cot, got[0] = fence(cot, got[0])
-    wire_g = over_all(dft_g(cot, bdt))
-    wire_g, kernel, pf, pi, got[1], got[2] = fence(wire_g, kernel, pf, pi, got[1], got[2])
-    modes_g = leg_g(wire_g, pi)
-    modes_g, got[3], got[4] = fence(modes_g, got[3], got[4])
-    coef_g = over_polar(modes_g.reshape(16, 16, 768))
-    coef_g, got[5] = fence(coef_g, got[5])
-    mixed_g = mix(coef_g, kernel, True)
-    mixed_g, got[0] = fence(mixed_g, got[0])
-    mixed_g = over_polar(mixed_g).reshape(DEG, 768)
-    wire_f = over_all(dft_f(me, got, bpt))
-
-    back_g = over_all(syn_g(mixed_g, pf))
-    modes_f = leg_f(wire_f, pf)
-    modes_f, back_g = fence(modes_f, back_g)
-    coef_f = over_polar(modes_f.reshape(16, 16, 768))
-
-    pieces = list(idft_g(me, back_g, bp))
-    pieces[0], coef_f = fence(pieces[0], coef_f)
-    mixed_f = over_polar(mix(coef_f, kernel, False)).reshape(DEG, 768)
-    got = hops(pieces, ORDER_E)
-    mixed_f, got[1], got[2], got[3], got[4] = fence(mixed_f, got[1], got[2], got[3], got[4])
-    back_f = over_all(syn_f(mixed_f, pi))
-    filtered = idft_f(back_f, bdt)
-    filtered, got[0] = fence(filtered, got[0])
+    wire = dft_f(me, got, bpt, dft_g(cot, bdt))
+    modes = leg(over_all(wire), pf, pi)
+    modes = over_polar(modes.reshape(16, 16, 1536))
+    modes = over_polar(mix(modes, kernel)).reshape(DEG, 1536)
+    back = over_all(syn(modes, pf, pi))
+
+    got = hops(list(idft_g(me, back, bp)), ORDER_E)
+    filtered = idft_f(back, bdt)
+    filtered, *got = fence(filtered, *got)
     return filtered.reshape(ROWS, 24, LON), post(me, got)
 
 

time: 267 us -> 279 us (1.045)
  blocking collectives: 0 us -> 57.4 us
  starting transfers between devices: 71.5 us -> 37.7 us
  local copies, waits for them, and re-layouts: 18.3 us -> 14.1 us
  Pallas kernels: 68.1 us -> 64.4 us
    all_to_all x0 -> x2, blocking collectives: none -> 57.4 us  [the longest x1 38.1 us: over_all(): return lax.all_to_all(x, both, 0, 0)]
    ppermute x14, waiting for transfers between devices: 25.6 us -> 68.9 us  [hop(): return lax.ppermute(piece, 'azimuth', [(a, a ^ s) for a in range(NA)])]
    all_to_all x4 -> x1, waiting for transfers between devices: 62.9 us -> 19.9 us  [over_all(): return lax.all_to_all(x, both, 0, 0)]
    all_to_all x4 -> x1, starting transfers between devices: 23.6 us -> 5.79 us  [over_polar(): return lax.all_to_all(x, 'polar', 0, 0)]
    all_to_all x4 -> x1, starting transfers between devices: 26.8 us -> 9.03 us  [over_all(): return lax.all_to_all(x, both, 0, 0)]
    pallas_call x8 -> x5, Pallas kernels: 41.8 us -> 36.6 us  [whole(): pl.pallas_call(body, out_shape=jax.ShapeDtypeStruct(out, BF), scratch_sha...]
    unnamed x33 -> x29, local copies, waits for them, and re-layouts: 5.02 us -> 1.68 us
    all_to_all x4 -> x1, waiting for transfers between devices: 10.7 us -> 9.96 us  [over_polar(): return lax.all_to_all(x, 'polar', 0, 0)]
  transfers between devices with their start and end apart: 22 -> 16, of which waited for: 10 -> 12; matrix products, arithmetic and copies ran while one was open for 7% -> 6% of each run, Pallas kernels for 19% -> 4%
where the time goes in v1:
time: 279 us; the launch traced here: 278 us
  waiting for transfers between devices  98.7 us (35%)
  Pallas kernels  64.4 us (23%)
  blocking collectives  57.4 us (21%)
  starting transfers between devices  37.7 us (14%)
  local copies, waits for them, and re-layouts  14.1 us (5%)
  other arithmetic  4.41 us (2%)
    ppermute x14, waiting for transfers between devices, hop(): return lax.ppermute(piece, 'azimuth', [(a, a ^ s) for a in range(NA)])  68.9 us
    all_to_all x1, blocking collectives, over_all(): return lax.all_to_all(x, both, 0, 0)  38.1 us
    pallas_call x5, Pallas kernels, whole(): pl.pallas_call(body, out_shape=jax.ShapeDtypeStruct(out, BF), scratch_sha...  36.6 us
    ppermute x14, starting transfers between devices, hop(): return lax.ppermute(piece, 'azimuth', [(a, a ^ s) for a in range(NA)])  22.9 us
    all_to_all x1, waiting for transfers between devices, over_all(): return lax.all_to_all(x, both, 0, 0)  19.9 us
    all_to_all x1, blocking collectives, over_polar(): return lax.all_to_all(x, 'polar', 0, 0)  19.3 us
    all_to_all x1, waiting for transfers between devices, over_polar(): return lax.all_to_all(x, 'polar', 0, 0)  9.96 us
    all_to_all x1, starting transfers between devices, over_all(): return lax.all_to_all(x, both, 0, 0)  9.03 us
  transfers between devices with their start and end apart: 16, of which 12 were waited for; matrix products, arithmetic and copies ran while one was open for 6% of the time, Pallas kernels for 4%

profile of v1, /device:TPU:1, one launch (start us, length us, event | category | flops | bytes accessed | tf_op | source)
XLA Modules:
  0.0 277.6 jit_solution(9281142197375321206)
XLA Ops:
  0.6 6.7 %prep.1 = (bf16[96,2304]{1,0:T(8,128)(2,1)}, bf16[96,2304]{1,0:T(8,128)(2,1)}, bf16[96,2304]{1,0:T(8,128)(2,1)}, bf16[96,2304]{1,0:T(8,128)(2,1)}, bf16[96,2304]...) custom-call(s32[1]{0:T(128)} %bitcast.me_ref, ...), custom_call_target="tpu_custom_call" | custom-call | tf_op jit(solution)/shard_map/prep/pallas_call | solution.py:76
  7.3 5.6 %collective-permute-start = (bf16[96,2304]{1,0:T(8,128)(2,1)}, bf16[96,2304]{1,0:T(8,128)(2,1)S(1)}, u32[]{:S(2)}, u32[]{:S(2)}) collective-permute-start(bf16[96,2304]{1,0:T(8,128)(2,1)} %get-tuple-element.31), channel_id=1, source_target_pairs={{0,7},{1,6},{2,5},{3,4},{4,3},{5,2},{6,1},{7,0},{8,15},{9,14},{10,... | collective-permute-start | bytes 1327112 | tf_op jit(solution)/shard_map/ppermute | solution.py:271
  14.8 2.4 collective-permute-start.4
  17.2 9.4 %collective-permute-done.refs_1_ = bf16[96,2304]{1,0:T(8,128)(2,1)S(1)} collective-permute-done((bf16[96,2304]{1,0:T(8,128)(2,1)}, bf16[96,2304]{1,0:T(8,128)(2,1)S(1)}, u32[]{:S(2)}, u32[]{:S(2)}) %collective-permute-start) | collective-permute-done | bytes 442400 | tf_op jit(solution)/shard_map/ppermute | solution.py:271
  26.6 2.1 collective-permute-start.5
  28.7 6.8 %collective-permute-done.1.refs_2_ = bf16[96,2304]{1,0:T(8,128)(2,1)S(1)} collective-permute-done((bf16[96,2304]{1,0:T(8,128)(2,1)}, bf16[96,2304]{1,0:T(8,128)(2,1)S(1)}, u32[]{:S(2)}, u32[]{:S(2)}) %collective-permute-start.1) | collective-permute-done | bytes 442400 | tf_op jit(solution)/shard_map/ppermute | solution.py:271
  36.0 5.7 %dft_g.1.refs_9_ = bf16[128,4,1152]{2,1,0:T(4,128)(2,1)} custom-call(bf16[1080,1440]{1,0:T(8,128)(2,1)} %bitcast.34, bf16[512,1440]{1,0:T(8,128)(2,1)} %constant.18.clone.b_ref), custom_call_target="tpu_custom_call" | custom-call | tf_op jit(solution)/shard_map/dft_g/pallas_call | solution.py:123
  41.6 3.0 %collective-permute-done.2.refs_3_ = bf16[96,2304]{1,0:T(8,128)(2,1)S(1)} collective-permute-done((bf16[96,2304]{1,0:T(8,128)(2,1)}, bf16[96,2304]{1,0:T(8,128)(2,1)S(1)}, u32[]{:S(2)}, u32[]{:S(2)}) %collective-permute-start.2) | collective-permute-done | bytes 442400 | tf_op jit(solution)/shard_map/ppermute | solution.py:271
  44.6 9.5 %collective-permute-done.3.refs_4_ = bf16[96,2304]{1,0:T(8,128)(2,1)S(1)} collective-permute-done((bf16[96,2304]{1,0:T(8,128)(2,1)}, bf16[96,2304]{1,0:T(8,128)(2,1)S(1)}, u32[]{:S(2)}, u32[]{:S(2)}) %collective-permute-start.3) | collective-permute-done | bytes 442400 | tf_op jit(solution)/shard_map/ppermute | solution.py:271
  54.1 6.3 %collective-permute-done.6.refs_7_ = bf16[96,2304]{1,0:T(8,128)(2,1)S(1)} collective-permute-done((bf16[96,2304]{1,0:T(8,128)(2,1)}, bf16[96,2304]{1,0:T(8,128)(2,1)S(1)}, u32[]{:S(2)}, u32[]{:S(2)}) %collective-permute-start.6) | collective-permute-done | bytes 442400 | tf_op jit(solution)/shard_map/ppermute | solution.py:271
  61.2 7.9 %dft_f.1 = bf16[128,8,1152]{2,1,0:T(8,128)(2,1)} custom-call(s32[1]{0:T(128)} %bitcast.me_ref, bf16[96,2304]{1,0:T(8,128)(2,1)} %get-tuple-element.30.refs_0_, bf16[96,2304]{1,0:T(8,128)(2,1)} %copy-done.1, bf16[96,2304]{1,0:T(8,128)(2,1)} %copy-done.3, bf16[96,2304]{1,0:T(8,128)(2,1)} %copy-done.5, bf16[96,2304]{1,0:T(8,128)(2,1)} %copy-done.7, ...), custom_call_target="tpu_custom_call" | custom-call | tf_op jit(solution)/shard_map/dft_f/pallas_call | solution.py:151
  69.1 9.0 %all-to-all-start = ((bf16[128,8,1152]{2,1,0:T(8,128)(2,1)}), bf16[128,8,1152]{2,1,0:T(8,128)(2,1)}, u32[]{:S(2)}, u32[]{:S(2)}) async-start(bf16[128,8,1152]{2,1,0:T(8,128)(2,1)} %dft_f.1), calls=%async_computation | async-start | bytes 4718592 | tf_op jit(solution)/shard_map/all_to_all | solution.py:287
  78.1 4.3 %constant_dynamic-slice_fusion = (bf16[720,2,256]{2,1,0:T(2,128)(2,1)S(1)}, bf16[720,2,256]{2,1,0:T(2,128)(2,1)S(1)}) fusion(bf16[720,16,256]{2,1,0:T(8,128)(2,1)} %param.11, s32[]{:T(128)S(6)} %select_n.4, bf16[720,16,256]{2,1,0:T(8,128)(2,1)} %param.10), kind=kLoop, calls=%fused_computation.5 | loop fusion | bytes 2949124 | tf_op jit(solution)/shard_map/dynamic_slice | solution.py:264
  85.7 4.8 %reshape.41 = bf16[16,2,192,192]{3,2,1,0:T(8,128)(2,1)S(1)} reshape(bf16[16,73728]{1,0:T(8,128)(2,1)} %param.12) | data formatting | bytes 4718592 | tf_op jit(solution)/shard_map/reshape | solution.py:299
  90.5 19.9 %all-to-all-done.r_ref = bf16[128,8,1152]{2,1,0:T(8,128)(2,1)} async-done(((bf16[128,8,1152]{2,1,0:T(8,128)(2,1)}), bf16[128,8,1152]{2,1,0:T(8,128)(2,1)}, u32[]{:S(2)}, u32[]{:S(2)}) %all-to-all-start) | async-done | bytes 2359328 | tf_op jit(solution)/shard_map/all_to_all | solution.py:287
  110.3 10.2 %leg.1 = bf16[256,1536]{1,0:T(8,128)(2,1)} custom-call(bf16[128,8,1152]{2,1,0:T(8,128)(2,1)} %all-to-all-done.r_ref, bf16[2,768,256]{2,1,0:T(8,128)(2,1)} %bitcast.29, bf16[2,768,256]{2,1,0:T(8,128)(2,1)} %bitcast.31), custom_call_target="tpu_custom_call" | custom-call | tf_op jit(solution)/shard_map/leg/pallas_call | solution.py:123
  120.5 5.8 %all-to-all-start.1 = ((bf16[16,16,1536]{2,1,0:T(8,128)(2,1)}), bf16[16,16,1536]{2,1,0:T(8,128)(2,1)}, u32[]{:S(2)}, u32[]{:S(2)}) async-start(bf16[16,16,1536]{2,1,0:T(8,128)(2,1)} %bitcast.35), calls=%async_computation.1 | async-start | bytes 1572864 | tf_op jit(solution)/shard_map/all_to_all | solution.py:290
  126.6 4.3 %maximum_maximum_fusion.k_ref = bf16[16,384,384]{2,1,0:T(8,128)(2,1)} fusion(bf16[16,192,192]{2,1,0:T(8,128)(2,1)S(1)} %get-tuple-element.57, bf16[16,192,192]{2,1,0:T(8,128)(2,1)S(1)} %fusion, bf16[16,192,192]{2,1,0:T(8,128)(2,1)S(1)} %get-tuple-element.56), kind=kLoop, calls=%fused_computation | loop fusion | flops 18874368 | bytes 8257536 | tf_op jit(solution)/shard_map/concatenate | solution.py:302
  130.9 10.0 %all-to-all-done.1.r_ref = bf16[16,16,1536]{2,1,0:T(8,128)(2,1)} async-done(((bf16[16,16,1536]{2,1,0:T(8,128)(2,1)}), bf16[16,16,1536]{2,1,0:T(8,128)(2,1)}, u32[]{:S(2)}, u32[]{:S(2)}) %all-to-all-start.1) | async-done | bytes 786464 | tf_op jit(solution)/shard_map/all_to_all | solution.py:290
  140.9 6.3 %mix.1 = bf16[16,16,1536]{2,1,0:T(8,128)(2,1)} custom-call(bf16[16,16,1536]{2,1,0:T(8,128)(2,1)} %all-to-all-done.1.r_ref, bf16[16,384,384]{2,1,0:T(8,128)(2,1)} %maximum_maximum_fusion.k_ref), custom_call_target="tpu_custom_call" | custom-call | tf_op jit(solution)/shard_map/mix/pallas_call | solution.py:123
  147.2 19.3 %all_to_all.20 = bf16[16,16,1536]{2,1,0:T(8,128)(2,1)} all-to-all(bf16[16,16,1536]{2,1,0:T(8,128)(2,1)} %mix.1), channel_id=1, replica_groups=mesh['polar'=16,'azimuth'=8] {'polar'}, dimensions={0} | all-to-all | bytes 1572864 | tf_op jit(solution)/shard_map/all_to_all | solution.py:290
  166.6 8.5 %syn.1 = bf16[128,8,1152]{2,1,0:T(8,128)(2,1)} custom-call(bf16[256,1536]{1,0:T(8,128)(2,1)} %bitcast.36, bf16[2,768,256]{2,1,0:T(8,128)(2,1)} %bitcast.30, bf16[2,768,256]{2,1,0:T(8,128)(2,1)} %bitcast.32), custom_call_target="tpu_custom_call" | custom-call | tf_op jit(solution)/shard_map/syn/pallas_call | solution.py:123
  175.1 38.1 %all_to_all.21.y_ref = bf16[128,8,1152]{2,1,0:T(8,128)(2,1)} all-to-all(bf16[128,8,1152]{2,1,0:T(8,128)(2,1)} %syn.1), channel_id=1, replica_groups=mesh['polar'=16,'azimuth'=8] {'polar','azimuth'}, dimensions={0} | all-to-all | bytes 4718592 | tf_op jit(solution)/shard_map/all_to_all | solution.py:287
  213.2 6.6 %idft_g.1 = (bf16[96,2304]{1,0:T(8,128)(2,1)}, bf16[96,2304]{1,0:T(8,128)(2,1)}, bf16[96,2304]{1,0:T(8,128)(2,1)}, bf16[96,2304]{1,0:T(8,128)(2,1)}, bf16[96,230...) custom-call(s32[1]{0:T(128)} %bitcast.me_ref, ...), custom_call_target="tpu_custom_call" | custom-call | tf_op jit(solution)/shard_map/idft_g/pallas_call | solution.py:252
  226.0 9.8 %collective-permute-done.10.refs_4_ = bf16[96,2304]{1,0:T(8,128)(2,1)S(1)} collective-permute-done((bf16[96,2304]{1,0:T(8,128)(2,1)}, bf16[96,2304]{1,0:T(8,128)(2,1)S(1)}, u32[]{:S(2)}, u32[]{:S(2)}) %collective-permute-start.10) | collective-permute-done | bytes 442400 | tf_op jit(solution)/shard_map/ppermute | solution.py:271
  235.8 4.3 %collective-permute-start.8 = (bf16[96,2304]{1,0:T(8,128)(2,1)}, bf16[96,2304]{1,0:T(8,128)(2,1)S(1)}, u32[]{:S(2)}, u32[]{:S(2)}) collective-permute-start(bf16[96,2304]{1,0:T(8,128)(2,1)} %get-tuple-element.41), channel_id=1, source_target_pairs={{0,3},{1,2},{2,1},{3,0},{4,7},{5,6},{6,5},{7,4},{8,11},{9,10},{10,... | collective-permute-start | bytes 1327112 | tf_op jit(solution)/shard_map/ppermute | solution.py:271
  240.1 5.3 %collective-permute-done.11.refs_5_ = bf16[96,2304]{1,0:T(8,128)(2,1)S(1)} collective-permute-done((bf16[96,2304]{1,0:T(8,128)(2,1)}, bf16[96,2304]{1,0:T(8,128)(2,1)S(1)}, u32[]{:S(2)}, u32[]{:S(2)}) %collective-permute-start.11) | collective-permute-done | bytes 442400 | tf_op jit(solution)/shard_map/ppermute | solution.py:271
  245.4 6.0 %idft_f.1 = bf16[1080,1440]{1,0:T(8,128)(2,1)} custom-call(bf16[128,8,1152]{2,1,0:T(8,128)(2,1)} %all_to_all.21.y_ref, bf16[512,1440]{1,0:T(8,128)(2,1)} %constant.18.clone.b_ref), custom_call_target="tpu_custom_call" | custom-call | tf_op jit(solution)/shard_map/idft_f/pallas_call | solution.py:123
  251.4 3.5 %collective-permute-done.12.refs_6_ = bf16[96,2304]{1,0:T(8,128)(2,1)S(1)} collective-permute-done((bf16[96,2304]{1,0:T(8,128)(2,1)}, bf16[96,2304]{1,0:T(8,128)(2,1)S(1)}, u32[]{:S(2)}, u32[]{:S(2)}) %collective-permute-start.12) | collective-permute-done | bytes 442400 | tf_op jit(solution)/shard_map/ppermute | solution.py:271
  254.9 10.5 %collective-permute-done.13.refs_7_ = bf16[96,2304]{1,0:T(8,128)(2,1)S(1)} collective-permute-done((bf16[96,2304]{1,0:T(8,128)(2,1)}, bf16[96,2304]{1,0:T(8,128)(2,1)S(1)}, u32[]{:S(2)}, u32[]{:S(2)}) %collective-permute-start.13) | collective-permute-done | bytes 442400 | tf_op jit(solution)/shard_map/ppermute | solution.py:271
  265.4 4.9 %collective-permute-done.9.refs_3_ = bf16[96,2304]{1,0:T(8,128)(2,1)S(1)} collective-permute-done((bf16[96,2304]{1,0:T(8,128)(2,1)}, bf16[96,2304]{1,0:T(8,128)(2,1)S(1)}, u32[]{:S(2)}, u32[]{:S(2)}) %collective-permute-start.9) | collective-permute-done | bytes 442400 | tf_op jit(solution)/shard_map/ppermute | solution.py:271
  271.0 6.6 %post.1 = bf16[45,34560]{1,0:T(8,128)(2,1)} custom-call(s32[1]{0:T(128)} %bitcast.me_ref, bf16[96,2304]{1,0:T(8,128)(2,1)} %get-tuple-element.48.refs_0_, bf16[96,2304]{1,0:T(8,128)(2,1)} %copy-done.8, bf16[96,2304]{1,0:T(8,128)(2,1)} %copy-done.10, bf16[96,2304]{1,0:T(8,128)(2,1)} %copy-done.12, bf16[96,2304]{1,0:T(8,128)(2,1)} %copy-done, ...), custom_call_target="tpu_custom_call" | custom-call | tf_op jit(solution)/shard_map/post/pallas_call | solution.py:107
  (49 shorter events, 13.7 us)
Async XLA Ops:
  7.3 19.2 %collective-permute-start = (bf16[96,2304]{1,0:T(8,128)(2,1)}, bf16[96,2304]{1,0:T(8,128)(2,1)S(1)}, u32[]{:S(2)}, u32[]{:S(2)}) collective-permute-start(bf16[96,2304]{1,0:T(8,128)(2,1)} %get-tuple-element.31), channel_id=1, source_target_pairs={{0,7},{1,6},{2,5},{3,4},{4,3},{5,2},{6,1},{7,0},{8,15},{9,14},{10,... | collective-permute-start | bytes 1327112 | tf_op jit(solution)/shard_map/ppermute | solution.py:271
  12.9 22.6 %collective-permute-start.1 = (bf16[96,2304]{1,0:T(8,128)(2,1)}, bf16[96,2304]{1,0:T(8,128)(2,1)S(1)}, u32[]{:S(2)}, u32[]{:S(2)}) collective-permute-start(bf16[96,2304]{1,0:T(8,128)(2,1)} %get-tuple-element.32), channel_id=1, source_target_pairs={{0,6},{1,7},{2,4},{3,5},{4,2},{5,3},{6,0},{7,1},{8,14},{9,15},{10,... | collective-permute-start | bytes 1327112 | tf_op jit(solution)/shard_map/ppermute | solution.py:271
  12.9 31.7 %collective-permute-start.2 = (bf16[96,2304]{1,0:T(8,128)(2,1)}, bf16[96,2304]{1,0:T(8,128)(2,1)S(1)}, u32[]{:S(2)}, u32[]{:S(2)}) collective-permute-start(bf16[96,2304]{1,0:T(8,128)(2,1)} %get-tuple-element.33), channel_id=1, source_target_pairs={{0,5},{1,4},{2,7},{3,6},{4,1},{5,0},{6,3},{7,2},{8,13},{9,12},{10,... | collective-permute-start | bytes 1327112 | tf_op jit(solution)/shard_map/ppermute | solution.py:271
  13.6 40.5 %collective-permute-start.3 = (bf16[96,2304]{1,0:T(8,128)(2,1)}, bf16[96,2304]{1,0:T(8,128)(2,1)S(1)}, u32[]{:S(2)}, u32[]{:S(2)}) collective-permute-start(bf16[96,2304]{1,0:T(8,128)(2,1)} %get-tuple-element.34), channel_id=1, source_target_pairs={{0,4},{1,5},{2,6},{3,7},{4,0},{5,1},{6,2},{7,3},{8,12},{9,13},{10,... | collective-permute-start | bytes 1327112 | tf_op jit(solution)/shard_map/ppermute | solution.py:271
  14.8 39.3 %collective-permute-start.4 = (bf16[96,2304]{1,0:T(8,128)(2,1)}, bf16[96,2304]{1,0:T(8,128)(2,1)S(1)}, u32[]{:S(2)}, u32[]{:S(2)}) collective-permute-start(bf16[96,2304]{1,0:T(8,128)(2,1)} %get-tuple-element.35), channel_id=1, source_target_pairs={{0,2},{1,3},{2,0},{3,1},{4,6},{5,7},{6,4},{7,5},{8,10},{9,11},{10,... | collective-permute-start | bytes 1327112 | tf_op jit(solution)/shard_map/ppermute | solution.py:271
  26.6 33.8 %copy-start.1 = (bf16[96,2304]{1,0:T(8,128)(2,1)}, bf16[96,2304]{1,0:T(8,128)(2,1)S(1)}, u32[]{:S(2)}) copy-start(bf16[96,2304]{1,0:T(8,128)(2,1)S(1)} %collective-permute-done.refs_1_) | copy-start | bytes 1327108
  26.6 27.5 %collective-permute-start.5 = (bf16[96,2304]{1,0:T(8,128)(2,1)}, bf16[96,2304]{1,0:T(8,128)(2,1)S(1)}, u32[]{:S(2)}, u32[]{:S(2)}) collective-permute-start(bf16[96,2304]{1,0:T(8,128)(2,1)} %get-tuple-element.36), channel_id=1, source_target_pairs={{0,3},{1,2},{2,1},{3,0},{4,7},{5,6},{6,5},{7,4},{8,11},{9,10},{10,... | collective-permute-start | bytes 1327112 | tf_op jit(solution)/shard_map/ppermute | solution.py:271
  35.5 24.9 %copy-start.3 = (bf16[96,2304]{1,0:T(8,128)(2,1)}, bf16[96,2304]{1,0:T(8,128)(2,1)S(1)}, u32[]{:S(2)}) copy-start(bf16[96,2304]{1,0:T(8,128)(2,1)S(1)} %collective-permute-done.1.refs_2_) | copy-start | bytes 1327108
  35.5 24.9 %collective-permute-start.6 = (bf16[96,2304]{1,0:T(8,128)(2,1)}, bf16[96,2304]{1,0:T(8,128)(2,1)S(1)}, u32[]{:S(2)}, u32[]{:S(2)}) collective-permute-start(bf16[96,2304]{1,0:T(8,128)(2,1)} %get-tuple-element.37), channel_id=1, source_target_pairs={{0,1},{1,0},{2,3},{3,2},{4,5},{5,4},{6,7},{7,6},{8,9},{9,8},{10,11... | collective-permute-start | bytes 1327112 | tf_op jit(solution)/shard_map/ppermute | solution.py:271
  44.6 15.8 %copy-start.5 = (bf16[96,2304]{1,0:T(8,128)(2,1)}, bf16[96,2304]{1,0:T(8,128)(2,1)S(1)}, u32[]{:S(2)}) copy-start(bf16[96,2304]{1,0:T(8,128)(2,1)S(1)} %collective-permute-done.2.refs_3_) | copy-start | bytes 1327108
  54.1 6.3 %copy-start.7 = (bf16[96,2304]{1,0:T(8,128)(2,1)}, bf16[96,2304]{1,0:T(8,128)(2,1)S(1)}, u32[]{:S(2)}) copy-start(bf16[96,2304]{1,0:T(8,128)(2,1)S(1)} %collective-permute-done.3.refs_4_) | copy-start | bytes 1327108
  54.1 6.3 %copy-start.9 = (bf16[96,2304]{1,0:T(8,128)(2,1)}, bf16[96,2304]{1,0:T(8,128)(2,1)S(1)}, u32[]{:S(2)}) copy-start(bf16[96,2304]{1,0:T(8,128)(2,1)S(1)} %collective-permute-done.4.refs_5_) | copy-start | bytes 1327108
  54.1 6.3 %copy-start.11 = (bf16[96,2304]{1,0:T(8,128)(2,1)}, bf16[96,2304]{1,0:T(8,128)(2,1)S(1)}, u32[]{:S(2)}) copy-start(bf16[96,2304]{1,0:T(8,128)(2,1)S(1)} %collective-permute-done.5.refs_6_) | copy-start | bytes 1327108
  60.4 0.8 copy-start.13
  69.1 41.3 %all-to-all-start = ((bf16[128,8,1152]{2,1,0:T(8,128)(2,1)}), bf16[128,8,1152]{2,1,0:T(8,128)(2,1)}, u32[]{:S(2)}, u32[]{:S(2)}) async-start(bf16[128,8,1152]{2,1,0:T(8,128)(2,1)} %dft_f.1), calls=%async_computation | async-start | bytes 4718592 | tf_op jit(solution)/shard_map/all_to_all | solution.py:287
  120.5 20.4 %all-to-all-start.1 = ((bf16[16,16,1536]{2,1,0:T(8,128)(2,1)}), bf16[16,16,1536]{2,1,0:T(8,128)(2,1)}, u32[]{:S(2)}, u32[]{:S(2)}) async-start(bf16[16,16,1536]{2,1,0:T(8,128)(2,1)} %bitcast.35), calls=%async_computation.1 | async-start | bytes 1572864 | tf_op jit(solution)/shard_map/all_to_all | solution.py:290
  219.8 16.0 %collective-permute-start.10 = (bf16[96,2304]{1,0:T(8,128)(2,1)}, bf16[96,2304]{1,0:T(8,128)(2,1)S(1)}, u32[]{:S(2)}, u32[]{:S(2)}) collective-permute-start(bf16[96,2304]{1,0:T(8,128)(2,1)} %get-tuple-element.43), channel_id=1, source_target_pairs={{0,7},{1,6},{2,5},{3,4},{4,3},{5,2},{6,1},{7,0},{8,15},{9,14},{10,... | collective-permute-start | bytes 1327112 | tf_op jit(solution)/shard_map/ppermute | solution.py:271
  221.5 23.9 %collective-permute-start.11 = (bf16[96,2304]{1,0:T(8,128)(2,1)}, bf16[96,2304]{1,0:T(8,128)(2,1)S(1)}, u32[]{:S(2)}, u32[]{:S(2)}) collective-permute-start(bf16[96,2304]{1,0:T(8,128)(2,1)} %get-tuple-element.44), channel_id=1, source_target_pairs={{0,6},{1,7},{2,4},{3,5},{4,2},{5,3},{6,0},{7,1},{8,14},{9,15},{10,... | collective-permute-start | bytes 1327112 | tf_op jit(solution)/shard_map/ppermute | solution.py:271
  222.2 32.7 %collective-permute-start.12 = (bf16[96,2304]{1,0:T(8,128)(2,1)}, bf16[96,2304]{1,0:T(8,128)(2,1)S(1)}, u32[]{:S(2)}, u32[]{:S(2)}) collective-permute-start(bf16[96,2304]{1,0:T(8,128)(2,1)} %get-tuple-element.45), channel_id=1, source_target_pairs={{0,5},{1,4},{2,7},{3,6},{4,1},{5,0},{6,3},{7,2},{8,13},{9,12},{10,... | collective-permute-start | bytes 1327112 | tf_op jit(solution)/shard_map/ppermute | solution.py:271
  224.1 41.3 %collective-permute-start.13 = (bf16[96,2304]{1,0:T(8,128)(2,1)}, bf16[96,2304]{1,0:T(8,128)(2,1)S(1)}, u32[]{:S(2)}, u32[]{:S(2)}) collective-permute-start(bf16[96,2304]{1,0:T(8,128)(2,1)} %get-tuple-element.46), channel_id=1, source_target_pairs={{0,4},{1,5},{2,6},{3,7},{4,0},{5,1},{6,2},{7,3},{8,12},{9,13},{10,... | collective-permute-start | bytes 1327112 | tf_op jit(solution)/shard_map/ppermute | solution.py:271
  225.1 40.2 %collective-permute-start.7 = (bf16[96,2304]{1,0:T(8,128)(2,1)}, bf16[96,2304]{1,0:T(8,128)(2,1)S(1)}, u32[]{:S(2)}, u32[]{:S(2)}) collective-permute-start(bf16[96,2304]{1,0:T(8,128)(2,1)} %get-tuple-element.40), channel_id=1, source_target_pairs={{0,2},{1,3},{2,0},{3,1},{4,6},{5,7},{6,4},{7,5},{8,10},{9,11},{10,... | collective-permute-start | bytes 1327112 | tf_op jit(solution)/shard_map/ppermute | solution.py:271
  235.8 15.6 %copy-start = (bf16[96,2304]{1,0:T(8,128)(2,1)}, bf16[96,2304]{1,0:T(8,128)(2,1)S(1)}, u32[]{:S(2)}) copy-start(bf16[96,2304]{1,0:T(8,128)(2,1)S(1)} %collective-permute-done.10.refs_4_) | copy-start | bytes 1327108
  235.8 29.6 %collective-permute-start.8 = (bf16[96,2304]{1,0:T(8,128)(2,1)}, bf16[96,2304]{1,0:T(8,128)(2,1)S(1)}, u32[]{:S(2)}, u32[]{:S(2)}) collective-permute-start(bf16[96,2304]{1,0:T(8,128)(2,1)} %get-tuple-element.41), channel_id=1, source_target_pairs={{0,3},{1,2},{2,1},{3,0},{4,7},{5,6},{6,5},{7,4},{8,11},{9,10},{10,... | collective-permute-start | bytes 1327112 | tf_op jit(solution)/shard_map/ppermute | solution.py:271
  245.4 6.0 %copy-start.2 = (bf16[96,2304]{1,0:T(8,128)(2,1)}, bf16[96,2304]{1,0:T(8,128)(2,1)S(1)}, u32[]{:S(2)}) copy-start(bf16[96,2304]{1,0:T(8,128)(2,1)S(1)} %collective-permute-done.11.refs_5_) | copy-start | bytes 1327108
  245.4 24.8 %collective-permute-start.9 = (bf16[96,2304]{1,0:T(8,128)(2,1)}, bf16[96,2304]{1,0:T(8,128)(2,1)S(1)}, u32[]{:S(2)}, u32[]{:S(2)}) collective-permute-start(bf16[96,2304]{1,0:T(8,128)(2,1)} %get-tuple-element.42), channel_id=1, source_target_pairs={{0,1},{1,0},{2,3},{3,2},{4,5},{5,4},{6,7},{7,6},{8,9},{9,8},{10,11... | collective-permute-start | bytes 1327112 | tf_op jit(solution)/shard_map/ppermute | solution.py:271
  254.9 15.4 %copy-start.4 = (bf16[96,2304]{1,0:T(8,128)(2,1)}, bf16[96,2304]{1,0:T(8,128)(2,1)S(1)}, u32[]{:S(2)}) copy-start(bf16[96,2304]{1,0:T(8,128)(2,1)S(1)} %collective-permute-done.12.refs_6_) | copy-start | bytes 1327108
  265.4 4.9 %copy-start.6 = (bf16[96,2304]{1,0:T(8,128)(2,1)}, bf16[96,2304]{1,0:T(8,128)(2,1)S(1)}, u32[]{:S(2)}) copy-start(bf16[96,2304]{1,0:T(8,128)(2,1)S(1)} %collective-permute-done.13.refs_7_) | copy-start | bytes 1327108
  265.4 4.9 %copy-start.8 = (bf16[96,2304]{1,0:T(8,128)(2,1)}, bf16[96,2304]{1,0:T(8,128)(2,1)S(1)}, u32[]{:S(2)}) copy-start(bf16[96,2304]{1,0:T(8,128)(2,1)S(1)} %collective-permute-done.7.refs_1_) | copy-start | bytes 1327108
  265.4 4.9 %copy-start.10 = (bf16[96,2304]{1,0:T(8,128)(2,1)}, bf16[96,2304]{1,0:T(8,128)(2,1)S(1)}, u32[]{:S(2)}) copy-start(bf16[96,2304]{1,0:T(8,128)(2,1)S(1)} %collective-permute-done.8.refs_2_) | copy-start | bytes 1327108
  270.2 0.8 copy-start.12
